TPU v7x, 32 devices: a whole 2x2x4 slice. The times are simulated.
32 devices in a mesh: pipe: 4 (over x, core), dp: 2 (over y), tensor: 4 (over z).
Axes of the slice: x: 2, y: 2, z: 4, core: 2. Of those that a mesh axis runs over, the one named last changes fastest.
Arguments:
- grad_top: bfloat16 [2, 128, 12288], P(None, None, ('dp', 'tensor')), may hold values from -1.1953125 to 1.1953125
- inputs: bfloat16 [4, 2, 128, 12288], P('pipe', None, None, ('dp', 'tensor')), may hold values from -6 to 6
- pre: bfloat16 [4, 2, 128, 6144], P('pipe', None, 'dp', 'tensor'), may hold values from -6 to 6
- weight_in: bfloat16 [4, 6144, 12288], P('pipe', 'tensor', 'dp'), may hold values from -0.0546875 to 0.0546875
- weight_out: bfloat16 [4, 6144, 12288], P('pipe', 'tensor', 'dp'), may hold values from -0.0546875 to 0.0546875
Outputs:
- weight_in_grad: bfloat16 [4, 6144, 12288], P('pipe', 'tensor', 'dp')
- weight_out_grad: bfloat16 [4, 6144, 12288], P('pipe', 'tensor', 'dp')
- section_grads: bfloat16 [4, 2, 128, 12288], P('pipe', None, None, ('dp', 'tensor'))
All inputs are finite; a program needn't handle non-finite values.
Results may differ from a plain program's by a relative error of at most 0.024.
Values may be sent and summed in bfloat16 or wider, within the bound.
A program may use at most 512 MiB of HBM per device.

v0:
```python
import math
import jax
import jax.numpy as jnp
from jax import lax
from jax.sharding import PartitionSpec as P


def shifted(block, axis, distance):
    devices = range(lax.axis_size(axis))
    route = [(i - distance, i) for i in devices if i - distance in devices]
    return lax.ppermute(block, axis, route)


def gelu_pair(values):
    root_coef = math.sqrt(2.0 / math.pi)
    inner = root_coef * (values + 0.044715 * values * values * values)
    tangent = jnp.tanh(inner)
    activ = 0.5 * values * (1.0 + tangent)
    slope = 0.5 * (1.0 + tangent) + 0.5 * values * (1.0 - tangent * tangent) * root_coef * (
        1.0 + 3.0 * 0.044715 * values * values
    )
    return (activ, slope)


def on_device(grad_top, inputs, pre, weight_in, weight_out):
    sections = lax.axis_size("pipe")
    section = lax.axis_index("pipe")
    micro = grad_top.shape[0]
    local_in = weight_in[0]
    local_out = weight_out[0]
    contract = (((0,), (0,)), ((), ()))
    accum_in = jnp.zeros(local_in.shape, jnp.float32)
    accum_out = jnp.zeros(local_out.shape, jnp.float32)
    grads_out = jnp.zeros(grad_top.shape, jnp.bfloat16)
    outgoing = grad_top[0]
    for timestep in range(micro + sections - 1):
        micro_index = timestep - (sections - 1 - section)
        valid = jnp.logical_and(micro_index >= 0, micro_index < micro)
        clipped = jnp.clip(micro_index, 0, micro - 1)
        top_grad = lax.dynamic_index_in_dim(grad_top, clipped, 0, False)
        if timestep == 0:
            current = top_grad
        else:
            received = shifted(outgoing, "pipe", -1)
            current = jnp.where(section == sections - 1, top_grad, received)
        layer_input = lax.dynamic_index_in_dim(inputs[0], clipped, 0, False)
        pre_local = lax.dynamic_index_in_dim(pre[0], clipped, 0, False)
        grad_cols, input_cols = (
            lax.all_gather(current, "tensor", axis=1, tiled=True),
            lax.all_gather(layer_input, "tensor", axis=1, tiled=True),
        )
        head_part = lax.dot_general(
            grad_cols, local_out, (((1,), (1,)), ((), ())), preferred_element_type=jnp.float32
        )
        head_grad = lax.psum(head_part.astype(jnp.bfloat16), "dp").astype(jnp.float32)
        pre_all = lax.all_gather(pre_local, "dp", axis=0, tiled=True)
        activ, slope = gelu_pair(pre_all.astype(jnp.float32))
        head_delta = (head_grad * slope).astype(jnp.bfloat16)
        activated = activ.astype(jnp.bfloat16)
        partial_value = jnp.dot(head_delta, local_in, preferred_element_type=jnp.float32)
        summed = lax.psum_scatter(
            partial_value.astype(jnp.bfloat16), "tensor", scatter_dimension=1, tiled=True
        ).astype(jnp.float32)
        new_grad = (current.astype(jnp.float32) + summed).astype(jnp.bfloat16)
        out_term = lax.dot_general(
            activated, grad_cols, contract, preferred_element_type=jnp.float32
        )
        in_term = lax.dot_general(
            head_delta, input_cols, contract, preferred_element_type=jnp.float32
        )
        accum_out = accum_out + jnp.where(valid, out_term, 0.0)
        accum_in = accum_in + jnp.where(valid, in_term, 0.0)
        previous = lax.dynamic_index_in_dim(grads_out, clipped, 0, False)
        grads_out = lax.dynamic_update_index_in_dim(
            grads_out, jnp.where(valid, new_grad, previous), clipped, 0
        )
        outgoing = new_grad
    return (
        accum_in.astype(jnp.bfloat16)[None],
        accum_out.astype(jnp.bfloat16)[None],
        grads_out[None],
    )


def solution(mesh):
    placed = (
        P(None, None, ("dp", "tensor")),
        P("pipe", None, None, ("dp", "tensor")),
        P("pipe", None, "dp", "tensor"),
        P("pipe", "tensor", "dp"),
        P("pipe", "tensor", "dp"),
    )
    return jax.shard_map(
        on_device,
        mesh=mesh,
        in_specs=placed,
        out_specs=(
            P("pipe", "tensor", "dp"),
            P("pipe", "tensor", "dp"),
            P("pipe", None, None, ("dp", "tensor")),
        ),
        check_vma=False,
    )
```

profile of v0, /device:TPU:0, one launch (start us, length us, event | category | flops | bytes accessed | tf_op | source)
XLA Modules:
  0.0 836.4 jit_solution(14600435980791823250)
XLA Ops:
  9.1 40.8 %all-gather.30.cloned.1.call-done = bf16[1,128,6144]{2,1,0:T(8,128)(2,1)} async-done(((bf16[1,128,1536]{2,1,0:T(8,128)(2,1)}), bf16[1,128,6144]{2,1,0:T(8,128)(2,1)}) %all-gather.30.cloned.1.call-update) | async-done | bytes 1572880 | tf_op jit(solution)/shard_map/all_gather | solution.py:49
  49.9 14.0 %fusion.37 = bf16[128,1536]{1,0:T(8,128)(2,1)} fusion(bf16[1,1536,6144]{2,1,0:T(8,128)(2,1)} %param.9, bf16[1,128,6144]{2,1,0:T(8,128)(2,1)} %all-gather.30.cloned.1.call-done), kind=kOutput, calls=%fused_computation.29 | convolution fusion | flops 2416115712 | bytes 20840448 | tf_op jit(solution)/shard_map/dot_general | solution.py:52
  74.2 15.2 %all-reduce.6.cloned.1.call-done = bf16[128,1536]{1,0:T(8,128)(2,1)} async-done(((bf16[128,1536]{1,0:T(8,128)(2,1)}), bf16[128,1536]{1,0:T(8,128)(2,1)}) %all-reduce.6.cloned.1.call-update) | async-done | bytes 393232 | tf_op jit(solution)/shard_map/psum | solution.py:55
  100.2 35.5 %reduce-scatter.6.cloned.1.call-done = bf16[128,1536]{1,0:T(8,128)(2,1)} async-done(((bf16[128,6144]{1,0:T(8,128)(2,1)}), bf16[128,1536]{1,0:T(8,128)(2,1)}) %reduce-scatter.6.cloned.1.call-update) | async-done | bytes 393232 | tf_op jit(solution)/shard_map/reduce_scatter | solution.py:61
  141.7 39.8 %all-gather.22.cloned.1.call-done = bf16[128,6144]{1,0:T(8,128)(2,1)} async-done(((bf16[128,1536]{1,0:T(8,128)(2,1)}), bf16[128,6144]{1,0:T(8,128)(2,1)}) %all-gather.22.cloned.1.call-update) | async-done | bytes 1572880 | tf_op jit(solution)/shard_map/all_gather | solution.py:49
  181.5 14.0 %fusion.40 = bf16[128,1536]{1,0:T(8,128)(2,1)} fusion(bf16[128,6144]{1,0:T(8,128)(2,1)} %all-gather.22.cloned.1.call-done, bf16[1,1536,6144]{2,1,0:T(8,128)(2,1)} %param.9), kind=kOutput, calls=%fused_computation.30 | convolution fusion | flops 2416115712 | bytes 20840448 | tf_op jit(solution)/shard_map/dot_general | solution.py:52
  203.8 16.6 %all-reduce.8.cloned.1.call-done = bf16[128,1536]{1,0:T(8,128)(2,1)} async-done(((bf16[128,1536]{1,0:T(8,128)(2,1)}), bf16[128,1536]{1,0:T(8,128)(2,1)}) %all-reduce.8.cloned.1.call-update) | async-done | bytes 393232 | tf_op jit(solution)/shard_map/psum | solution.py:55
  220.4 10.7 %fusion.25 = bf16[128,6144]{1,0:T(8,128)(2,1)} fusion(bf16[1,1536,6144]{2,1,0:T(8,128)(2,1)} %param.8, bf16[128,1536]{1,0:T(8,128)(2,1)} %all-reduce.8.cloned.1.call-done, bf16[1,1,128,1536]{3,2,1,0:T(8,128)(2,1)S(1)} %all-gather.3), kind=kOutput, calls=%fused_computation.25 | convolution fusion | flops 2420834304 | bytes 21233664 | tf_op jit(solution)/shard_map/dot_general | solution.py:60
  231.2 35.5 %reduce-scatter.8.cloned.1.call-done = bf16[128,1536]{1,0:T(8,128)(2,1)} async-done(((bf16[128,6144]{1,0:T(8,128)(2,1)}), bf16[128,1536]{1,0:T(8,128)(2,1)}) %reduce-scatter.8.cloned.1.call-update) | async-done | bytes 393232 | tf_op jit(solution)/shard_map/reduce_scatter | solution.py:61
  272.9 39.5 %all-gather.24.cloned.1.call-done = bf16[128,6144]{1,0:T(8,128)(2,1)} async-done(((bf16[128,1536]{1,0:T(8,128)(2,1)}), bf16[128,6144]{1,0:T(8,128)(2,1)}) %all-gather.24.cloned.1.call-update) | async-done | bytes 1572880 | tf_op jit(solution)/shard_map/all_gather | solution.py:49
  312.4 14.0 %fusion.43 = bf16[128,1536]{1,0:T(8,128)(2,1)} fusion(bf16[128,6144]{1,0:T(8,128)(2,1)} %all-gather.24.cloned.1.call-done, bf16[1,1536,6144]{2,1,0:T(8,128)(2,1)} %param.9), kind=kOutput, calls=%fused_computation.31 | convolution fusion | flops 2416115712 | bytes 20840448 | tf_op jit(solution)/shard_map/dot_general | solution.py:52
  334.7 16.6 %all-reduce.10.cloned.1.call-done = bf16[128,1536]{1,0:T(8,128)(2,1)} async-done(((bf16[128,1536]{1,0:T(8,128)(2,1)}), bf16[128,1536]{1,0:T(8,128)(2,1)}) %all-reduce.10.cloned.1.call-update) | async-done | bytes 393232 | tf_op jit(solution)/shard_map/psum | solution.py:55
  362.1 35.5 %reduce-scatter.10.cloned.1.call-done = bf16[128,1536]{1,0:T(8,128)(2,1)} async-done(((bf16[128,6144]{1,0:T(8,128)(2,1)}), bf16[128,1536]{1,0:T(8,128)(2,1)}) %reduce-scatter.10.cloned.1.call-update) | async-done | bytes 393232 | tf_op jit(solution)/shard_map/reduce_scatter | solution.py:61
  403.4 39.9 %all-gather.26.cloned.1.call-done = bf16[128,6144]{1,0:T(8,128)(2,1)} async-done(((bf16[128,1536]{1,0:T(8,128)(2,1)}), bf16[128,6144]{1,0:T(8,128)(2,1)}) %all-gather.26.cloned.1.call-update) | async-done | bytes 1572880 | tf_op jit(solution)/shard_map/all_gather | solution.py:49
  443.3 14.0 %fusion.46 = bf16[128,1536]{1,0:T(8,128)(2,1)} fusion(bf16[128,6144]{1,0:T(8,128)(2,1)} %all-gather.26.cloned.1.call-done, bf16[1,1536,6144]{2,1,0:T(8,128)(2,1)} %param.9), kind=kOutput, calls=%fused_computation.32 | convolution fusion | flops 2416115712 | bytes 20840448 | tf_op jit(solution)/shard_map/dot_general | solution.py:52
  465.2 16.9 %all-reduce.12.cloned.1.call-done = bf16[128,1536]{1,0:T(8,128)(2,1)} async-done(((bf16[128,1536]{1,0:T(8,128)(2,1)}), bf16[128,1536]{1,0:T(8,128)(2,1)}) %all-reduce.12.cloned.1.call-update) | async-done | bytes 393232 | tf_op jit(solution)/shard_map/psum | solution.py:55
  482.1 10.7 %fusion.31 = bf16[128,6144]{1,0:T(8,128)(2,1)} fusion(bf16[1,1536,6144]{2,1,0:T(8,128)(2,1)} %param.8, bf16[128,1536]{1,0:T(8,128)(2,1)} %all-reduce.12.cloned.1.call-done, bf16[1,1,128,1536]{3,2,1,0:T(8,128)(2,1)S(1)} %all-gather.7), kind=kOutput, calls=%fused_computation.27 | convolution fusion | flops 2420834304 | bytes 21233664 | tf_op jit(solution)/shard_map/dot_general | solution.py:60
  493.6 34.8 %reduce-scatter.12.cloned.1.call-done = bf16[128,1536]{1,0:T(8,128)(2,1)} async-done(((bf16[128,6144]{1,0:T(8,128)(2,1)}), bf16[128,1536]{1,0:T(8,128)(2,1)}) %reduce-scatter.12.cloned.1.call-update) | async-done | bytes 393232 | tf_op jit(solution)/shard_map/reduce_scatter | solution.py:61
  539.2 35.2 %all-gather.28.cloned.1.call-done = bf16[128,6144]{1,0:T(8,128)(2,1)} async-done(((bf16[128,1536]{1,0:T(8,128)(2,1)}), bf16[128,6144]{1,0:T(8,128)(2,1)}) %all-gather.28.cloned.1.call-update) | async-done | bytes 1572880 | tf_op jit(solution)/shard_map/all_gather | solution.py:49
  574.3 14.0 %fusion.49 = bf16[128,1536]{1,0:T(8,128)(2,1)} fusion(bf16[128,6144]{1,0:T(8,128)(2,1)} %all-gather.28.cloned.1.call-done, bf16[1,1536,6144]{2,1,0:T(8,128)(2,1)} %param.9), kind=kOutput, calls=%fused_computation.33 | convolution fusion | flops 2416115712 | bytes 20840448 | tf_op jit(solution)/shard_map/dot_general | solution.py:52
  595.9 14.9 %fusion.61 = f32[1536,6144]{1,0:T(8,128)} fusion(bf16[1,128,6144]{2,1,0:T(8,128)(2,1)S(1)} %copy-done.2, bf16[1,1,128,1536]{3,2,1,0:T(8,128)(2,1)S(1)} %all-gather.1), kind=kOutput, calls=%fused_computation.78 | convolution fusion | flops 2417885184 | bytes 39714816 | tf_op jit(solution)/shard_map/dot_general | solution.py:65
  611.7 16.8 %fusion.59 = f32[1536,6144]{1,0:T(8,128)} fusion(bf16[1,1,128,6144]{3,2,1,0:T(8,128)(2,1)} %all-gather.32.cloned.1.call-done, bf16[128,1536]{1,0:T(8,128)(2,1)} %all-reduce.6.cloned.1.call-done, bf16[1,1,128,1536]{3,2,1,0:T(8,128)(2,1)S(1)} %all-gather.1), kind=kOutput, calls=%fused_computation.76 | convolution fusion | flops 2420047872 | bytes 40108032 | tf_op jit(solution)/shard_map/dot_general | solution.py:68
  628.5 14.9 %fusion.121 = f32[1536,6144]{1,0:T(8,128)} fusion(bf16[128,6144]{1,0:T(8,128)(2,1)S(1)} %copy-done.3, bf16[1,1,128,1536]{3,2,1,0:T(8,128)(2,1)S(1)} %copy-done.7), kind=kOutput, calls=%fused_computation.142 | convolution fusion | flops 2417885184 | bytes 39714816 | tf_op jit(solution)/shard_map/dot_general | solution.py:65
  649.6 16.7 %fusion.57 = f32[1536,6144]{1,0:T(8,128)} fusion(bf16[1,1,128,6144]{3,2,1,0:T(8,128)(2,1)} %all-gather.34.cloned.1.call-done, bf16[128,1536]{1,0:T(8,128)(2,1)S(1)} %copy-done.20, bf16[1,1,128,1536]{3,2,1,0:T(8,128)(2,1)S(1)} %copy-done.7), kind=kOutput, calls=%fused_computation.74 | convolution fusion | flops 2420047872 | bytes 40108032 | tf_op jit(solution)/shard_map/dot_general | solution.py:68
  666.3 15.4 %fusion.123 = f32[1536,6144]{1,0:T(8,128)} fusion(bf16[128,6144]{1,0:T(8,128)(2,1)S(1)} %copy-done.4, bf16[1,1,128,1536]{3,2,1,0:T(8,128)(2,1)S(1)} %copy-done.9), kind=kOutput, calls=%fused_computation.143 | convolution fusion | flops 2417885184 | bytes 39714816 | tf_op jit(solution)/shard_map/dot_general | solution.py:65
  687.5 16.6 %fusion.55 = f32[1536,6144]{1,0:T(8,128)} fusion(bf16[1,1,128,6144]{3,2,1,0:T(8,128)(2,1)} %all-gather.36.cloned.1.call-done, bf16[128,1536]{1,0:T(8,128)(2,1)S(1)} %copy-done.21, bf16[1,1,128,1536]{3,2,1,0:T(8,128)(2,1)S(1)} %copy-done.9), kind=kOutput, calls=%fused_computation.72 | convolution fusion | flops 2420047872 | bytes 40108032 | tf_op jit(solution)/shard_map/dot_general | solution.py:68
  704.1 14.9 %fusion.125 = f32[1536,6144]{1,0:T(8,128)} fusion(bf16[128,6144]{1,0:T(8,128)(2,1)S(1)} %copy-done.5, bf16[1,1,128,1536]{3,2,1,0:T(8,128)(2,1)S(1)} %copy-done.11), kind=kOutput, calls=%fused_computation.144 | convolution fusion | flops 2417885184 | bytes 39714816 | tf_op jit(solution)/shard_map/dot_general | solution.py:65
  724.8 16.4 %fusion.53 = f32[1536,6144]{1,0:T(8,128)} fusion(bf16[1,1,128,6144]{3,2,1,0:T(8,128)(2,1)} %all-gather.38.cloned.1.call-done, bf16[128,1536]{1,0:T(8,128)(2,1)S(1)} %copy-done.22, bf16[1,1,128,1536]{3,2,1,0:T(8,128)(2,1)S(1)} %copy-done.11), kind=kOutput, calls=%fused_computation.70 | convolution fusion | flops 2420047872 | bytes 40108032 | tf_op jit(solution)/shard_map/dot_general | solution.py:68
  742.1 25.1 %fusion.1 = bf16[1,1536,6144]{2,1,0:T(8,128)(2,1)} fusion(bf16[128,6144]{1,0:T(8,128)(2,1)S(1)} %copy-done.1, f32[1536,6144]{1,0:T(8,128)} %fusion.125, f32[1536,6144]{1,0:T(8,128)} %fusion.123, f32[1536,6144]{1,0:T(8,128)} %fusion.121, f32[1536,6144]{1,0:T(8,128)} %fusion.61, pred[]{:T(512)S(6)} %and.20, pred[]{:T(512)S(6)} %and.19, pred[]{:T(512)S(6)} %and.18, ...), kind=kOutput, calls=%fused_computation.3 | convolution fusion | flops 2512257024 | bytes 171835392 | tf_op jit(solution)/shard_map/dot_general | solution.py:65
  767.3 10.8 %fusion.34 = bf16[128,6144]{1,0:T(8,128)(2,1)} fusion(bf16[1,1536,6144]{2,1,0:T(8,128)(2,1)} %param.8, bf16[128,1536]{1,0:T(8,128)(2,1)} %all-reduce.14.cloned.1.call-done, bf16[1,1,128,1536]{3,2,1,0:T(8,128)(2,1)S(1)} %copy-done.15), kind=kOutput, calls=%fused_computation.28 | convolution fusion | flops 2420834304 | bytes 21233664 | tf_op jit(solution)/shard_map/dot_general | solution.py:60
  778.1 12.7 %all-gather.40.cloned.1.call-done = bf16[1,1,128,6144]{3,2,1,0:T(8,128)(2,1)} async-done(((bf16[1,1,128,1536]{3,2,1,0:T(8,128)(2,1)}), bf16[1,1,128,6144]{3,2,1,0:T(8,128)(2,1)}) %all-gather.40.cloned.1.call-update) | async-done | bytes 1572880 | tf_op jit(solution)/shard_map/all_gather | solution.py:50
  790.9 25.9 %fusion = bf16[1,1536,6144]{2,1,0:T(8,128)(2,1)} fusion(f32[1536,6144]{1,0:T(8,128)} %fusion.53, f32[1536,6144]{1,0:T(8,128)} %fusion.55, f32[1536,6144]{1,0:T(8,128)} %fusion.57, f32[1536,6144]{1,0:T(8,128)} %fusion.59, pred[]{:T(512)S(6)} %and.20, pred[]{:T(512)S(6)} %and.19, pred[]{:T(512)S(6)} %and.18, pred[]{:T(512)S(6)} %and.17, pred[]{:T(512)S(6)} %and.16, ...), kind=kOutput, calls=%fused_computation.2 | convolution fusion | flops 2514419712 | bytes 172228608 | tf_op jit(solution)/shard_map/dot_general | solution.py:68
  (126 shorter events, 127.6 us)
Async XLA Ops:
  7.2 56.8 %copy-start.16 = (bf16[1,2,64,1536]{3,2,1,0:T(8,128)(2,1)S(1)}, bf16[1,2,64,1536]{3,2,1,0:T(8,128)(2,1)}, u32[]{:S(2)}) copy-start(bf16[1,2,64,1536]{3,2,1,0:T(8,128)(2,1)} %param.7) | copy-start | bytes 1179652
  7.2 42.7 %all-gather.30.cloned.1.call-start = ((), (), s32[]{:S(2)}) async-start(), calls=%async_computation.19 | async-start | bytes 1966080 | tf_op jit(solution)/shard_map/all_gather | solution.py:49
  9.1 80.4 %all-reduce.6.cloned.1.call-start = ((), (), s32[]{:S(2)}) async-start(), calls=%async_computation.5 | async-start | bytes 786432 | tf_op jit(solution)/shard_map/psum | solution.py:55
  63.9 71.9 %copy-start = (bf16[2,128,1536]{2,1,0:T(8,128)(2,1)S(1)}, bf16[2,128,1536]{2,1,0:T(8,128)(2,1)}, u32[]{:S(2)}) copy-start(bf16[2,128,1536]{2,1,0:T(8,128)(2,1)} %param.5) | copy-start | bytes 2359300
  63.9 71.9 %reduce-scatter.6.cloned.1.call-start = ((), (), s32[]{:S(2)}) async-start(), calls=%async_computation.6 | async-start | bytes 1966080 | tf_op jit(solution)/shard_map/reduce_scatter | solution.py:61
  100.2 81.4 %all-gather.22.cloned.1.call-start = ((), (), s32[]{:S(2)}) async-start(), calls=%async_computation.7 | async-start | bytes 1966080 | tf_op jit(solution)/shard_map/all_gather | solution.py:49
  137.0 3.6 collective-permute-start
  141.4 79.0 %all-reduce.8.cloned.1.call-start = ((), (), s32[]{:S(2)}) async-start(), calls=%async_computation.8 | async-start | bytes 786432 | tf_op jit(solution)/shard_map/psum | solution.py:55
  195.5 71.2 %copy-start.12 = (bf16[128,1536]{1,0:T(8,128)(2,1)S(1)}, bf16[128,1536]{1,0:T(8,128)(2,1)}, u32[]{:S(2)}) copy-start(bf16[128,1536]{1,0:T(8,128)(2,1)} %bitcast_select_fusion.6) | copy-start | bytes 1179652
  195.5 71.2 %reduce-scatter.8.cloned.1.call-start = ((), (), s32[]{:S(2)}) async-start(), calls=%async_computation.9 | async-start | bytes 1966080 | tf_op jit(solution)/shard_map/reduce_scatter | solution.py:61
  203.8 122.6 %copy-start.6 = (bf16[1,1,128,1536]{3,2,1,0:T(8,128)(2,1)}, bf16[1,1,128,1536]{3,2,1,0:T(8,128)(2,1)S(1)}, u32[]{:S(2)}) copy-start(bf16[1,1,128,1536]{3,2,1,0:T(8,128)(2,1)S(1)} %all-gather.3) | copy-start | bytes 1179652
  231.1 81.3 %all-gather.24.cloned.1.call-start = ((), (), s32[]{:S(2)}) async-start(), calls=%async_computation.10 | async-start | bytes 1966080 | tf_op jit(solution)/shard_map/all_gather | solution.py:49
  267.9 3.6 collective-permute-start.1
  272.3 79.0 %all-reduce.10.cloned.1.call-start = ((), (), s32[]{:S(2)}) async-start(), calls=%async_computation.11 | async-start | bytes 786432 | tf_op jit(solution)/shard_map/psum | solution.py:55
  326.4 71.2 %copy-start.13 = (bf16[128,1536]{1,0:T(8,128)(2,1)S(1)}, bf16[128,1536]{1,0:T(8,128)(2,1)}, u32[]{:S(2)}) copy-start(bf16[128,1536]{1,0:T(8,128)(2,1)} %bitcast_select_fusion.5) | copy-start | bytes 1179652
  326.4 71.2 %reduce-scatter.10.cloned.1.call-start = ((), (), s32[]{:S(2)}) async-start(), calls=%async_computation.12 | async-start | bytes 1966080 | tf_op jit(solution)/shard_map/reduce_scatter | solution.py:61
  334.7 122.5 %copy-start.8 = (bf16[1,1,128,1536]{3,2,1,0:T(8,128)(2,1)}, bf16[1,1,128,1536]{3,2,1,0:T(8,128)(2,1)S(1)}, u32[]{:S(2)}) copy-start(bf16[1,1,128,1536]{3,2,1,0:T(8,128)(2,1)S(1)} %all-gather.5) | copy-start | bytes 1179652
  362.0 81.3 %all-gather.26.cloned.1.call-start = ((), (), s32[]{:S(2)}) async-start(), calls=%async_computation.13 | async-start | bytes 1966080 | tf_op jit(solution)/shard_map/all_gather | solution.py:49
  398.8 3.6 collective-permute-start.2
  403.2 78.9 %all-reduce.12.cloned.1.call-start = ((), (), s32[]{:S(2)}) async-start(), calls=%async_computation.14 | async-start | bytes 786432 | tf_op jit(solution)/shard_map/psum | solution.py:55
  457.3 71.1 %reduce-scatter.12.cloned.1.call-start = ((), (), s32[]{:S(2)}) async-start(), calls=%async_computation.15 | async-start | bytes 1966080 | tf_op jit(solution)/shard_map/reduce_scatter | solution.py:61
  492.7 103.2 %copy-start.2 = (bf16[1,128,6144]{2,1,0:T(8,128)(2,1)S(1)}, bf16[1,128,6144]{2,1,0:T(8,128)(2,1)}, u32[]{:S(2)}) copy-start(bf16[1,128,6144]{2,1,0:T(8,128)(2,1)} %all-gather.30.cloned.1.call-done) | copy-start | bytes 4718596
  492.8 81.5 %all-gather.28.cloned.1.call-start = ((), (), s32[]{:S(2)}) async-start(), calls=%async_computation.16 | async-start | bytes 1966080 | tf_op jit(solution)/shard_map/all_gather | solution.py:49
  529.8 3.6 collective-permute-start.3
  534.2 55.0 %copy-start.19 = (bf16[1,1,64,1536]{3,2,1,0:T(8,128)(2,1)S(1)}, bf16[1,1,64,1536]{3,2,1,0:T(8,128)(2,1)}, u32[]{:S(2)}) copy-start(bf16[1,1,64,1536]{3,2,1,0:T(8,128)(2,1)} %get-tuple-element.16) | copy-start | bytes 589828
  534.2 77.5 %all-gather.32.cloned.1.call-start = ((), (), s32[]{:S(2)}) async-start(), calls=%async_computation.20 | async-start | bytes 1966080 | tf_op jit(solution)/shard_map/all_gather | solution.py:50
  537.4 112.2 %all-gather.34.cloned.1.call-start = ((), (), s32[]{:S(2)}) async-start(), calls=%async_computation.21 | async-start | bytes 1966080 | tf_op jit(solution)/shard_map/all_gather | solution.py:50
  538.0 149.5 %all-gather.36.cloned.1.call-start = ((), (), s32[]{:S(2)}) async-start(), calls=%async_computation.22 | async-start | bytes 1966080 | tf_op jit(solution)/shard_map/all_gather | solution.py:50
  538.5 186.3 %all-gather.38.cloned.1.call-start = ((), (), s32[]{:S(2)}) async-start(), calls=%async_computation.23 | async-start | bytes 1966080 | tf_op jit(solution)/shard_map/all_gather | solution.py:50
  539.1 228.1 %all-reduce.14.cloned.1.call-start = ((), (), s32[]{:S(2)}) async-start(), calls=%async_computation.17 | async-start | bytes 786432 | tf_op jit(solution)/shard_map/psum | solution.py:55
  588.4 202.5 %all-gather.40.cloned.1.call-start = ((), (), s32[]{:S(2)}) async-start(), calls=%async_computation.24 | async-start | bytes 1966080 | tf_op jit(solution)/shard_map/all_gather | solution.py:50
  589.1 238.2 %reduce-scatter.14.cloned.1.call-start = ((), (), s32[]{:S(2)}) async-start(), calls=%async_computation.18 | async-start | bytes 1966080 | tf_op jit(solution)/shard_map/reduce_scatter | solution.py:61
  (16 other events, 375.3 us)
Sparse Core Ops, SparseCore 0:
  10.1 39.7 all-gather.29
  64.0 25.3 all-reduce.5
  100.3 35.4 reduce-scatter.5
  141.5 39.9 all-gather.21
  195.6 24.7 all-reduce.7
  231.2 35.4 reduce-scatter.7
  272.4 39.9 all-gather.23
  326.5 24.7 all-reduce.9
  362.1 35.4 reduce-scatter.9
  403.3 39.9 all-gather.25
  457.4 24.6 all-reduce.11
  492.9 35.4 reduce-scatter.11
  534.3 39.9 all-gather.27
  575.7 35.8 all-gather.31
  613.6 35.8 all-gather.33
  651.6 35.8 all-gather.35
  688.9 35.8 all-gather.37
  727.0 24.6 all-reduce.13
  753.8 37.0 all-gather.39
  793.0 34.2 reduce-scatter.13
where the time goes:
time: 843 us; the launch traced here: 836 us
  waiting for transfers between devices  456 us (54%)
  matrix products  301 us (36%)
  blocking collectives  40.5 us (5%)
  between operations  14.8 us (2%)
  other arithmetic  9.16 us (1%)
  local copies, waits for them, and re-layouts  8.44 us (1%)
    all_gather x5, waiting for transfers between devices, on_device(): lax.all_gather(current, 'tensor', axis=1, tiled=True)  195 us
    reduce_scatter x5, waiting for transfers between devices, on_device(): lax.psum_scatter(partial_value.astype(jnp.bfloat16), 'tensor', scatter_di...  152 us
    dot_general x5, matrix products, on_device(): lax.dot_general(head_delta, input_cols, contract, preferred_element_type=...  92.4 us
    dot_general x5, matrix products, on_device(): lax.dot_general(activated, grad_cols, contract, preferred_element_type=jn...  85.1 us
    dot_general x5, matrix products, on_device(): lax.dot_general(grad_cols, local_out, (((1,), (1,)), ((), ())), preferred...  69.8 us
    psum x5, waiting for transfers between devices, on_device(): lax.psum(head_part.astype(jnp.bfloat16), 'dp').astype(jnp.float32)  65.3 us
    dot_general x5, matrix products, on_device(): jnp.dot(head_delta, local_in, preferred_element_type=jnp.float32)  53.6 us
    all_gather x5, blocking collectives, on_device(): pre_all = lax.all_gather(pre_local, 'dp', axis=0, tiled=True)  40.5 us
  transfers between devices with their start and end apart: 24, of which 23 were waited for; matrix products, arithmetic and copies ran while one was open for 25% of the time, Pallas kernels for 0%

commit v1 on v0

--- a/solution.py
+++ b/solution.py
@@ -3,6 +3,27 @@
 import jax.numpy as jnp
 from jax import lax
 from jax.sharding import PartitionSpec as P
+
+
+def gather_around(x, axis, dim):
+    size, position, rows = (lax.axis_size(axis), lax.axis_index(axis), x.shape[dim])
+    forward = [(i, (i + 1) % size) for i in range(size)]
+    behind = [(i, (i - 1) % size) for i in range(size)]
+    whole = jnp.zeros((*x.shape[:dim], size * rows, *x.shape[dim + 1 :]), x.dtype)
+    whole = lax.dynamic_update_slice_in_dim(whole, x, position * rows, axis=dim)
+    from_left = from_right = x
+    halfway = size // 2
+    for step in range(1, halfway + 1):
+        from_left = lax.ppermute(from_left, axis, forward)
+        whole = lax.dynamic_update_slice_in_dim(
+            whole, from_left, (position - step) % size * rows, axis=dim
+        )
+        if step < size - halfway:
+            from_right = lax.ppermute(from_right, axis, behind)
+            whole = lax.dynamic_update_slice_in_dim(
+                whole, from_right, (position + step) % size * rows, axis=dim
+            )
+    return whole
 
 
 def shifted(block, axis, distance):
@@ -46,7 +67,7 @@
         layer_input = lax.dynamic_index_in_dim(inputs[0], clipped, 0, False)
         pre_local = lax.dynamic_index_in_dim(pre[0], clipped, 0, False)
         grad_cols, input_cols = (
-            lax.all_gather(current, "tensor", axis=1, tiled=True),
+            gather_around(current, "tensor", 1),
             lax.all_gather(layer_input, "tensor", axis=1, tiled=True),
         )
         head_part = lax.dot_general(

time: 843 us -> 794 us (0.942)
  waiting for transfers between devices: 456 us -> 375 us
  starting transfers between devices: 6.98 us -> 36.3 us
    all_gather x5 -> x0, waiting for transfers between devices: 195 us -> none  [on_device(): lax.all_gather(current, 'tensor', axis=1, tiled=True)]
    ppermute x0 -> x15, waiting for transfers between devices: none -> 133 us  [the longest x10 90.2 us: gather_around(): from_left = lax.ppermute(from_left, axis, forward)]
    all_gather x5, waiting for transfers between devices: 31.5 us -> 0.03 us  [on_device(): lax.all_gather(layer_input, 'tensor', axis=1, tiled=True)]
    ppermute x0 -> x15, starting transfers between devices: none -> 30.5 us  [the longest x5 16.8 us: gather_around(): from_right = lax.ppermute(from_right, axis, behind)]
    psum x5, waiting for transfers between devices: 65.3 us -> 80.3 us  [on_device(): lax.psum(head_part.astype(jnp.bfloat16), 'dp').astype(jnp.float32)]
  transfers between devices with their start and end apart: 24 -> 34, of which waited for: 23 -> 28; matrix products, arithmetic and copies ran while one was open for 25% -> 27% of each run, Pallas kernels for 0% -> 0%
where the time goes in v1:
time: 794 us; the launch traced here: 784 us
  waiting for transfers between devices  375 us (47%)
  matrix products  302 us (38%)
  blocking collectives  37 us (5%)
  starting transfers between devices  36.3 us (5%)
  between operations  14.8 us (2%)
  local copies, waits for them, and re-layouts  9.64 us (1%)
  other arithmetic  9.35 us (1%)
    reduce_scatter x5, waiting for transfers between devices, on_device(): lax.psum_scatter(partial_value.astype(jnp.bfloat16), 'tensor', scatter_di...  150 us
    dot_general x5, matrix products, on_device(): lax.dot_general(head_delta, input_cols, contract, preferred_element_type=...  93.1 us
    ppermute x10, waiting for transfers between devices, gather_around(): from_left = lax.ppermute(from_left, axis, forward)  90.2 us
    dot_general x5, matrix products, on_device(): lax.dot_general(activated, grad_cols, contract, preferred_element_type=jn...  86.2 us
    psum x5, waiting for transfers between devices, on_device(): lax.psum(head_part.astype(jnp.bfloat16), 'dp').astype(jnp.float32)  80.3 us
    dot_general x5, matrix products, on_device(): lax.dot_general(grad_cols, local_out, (((1,), (1,)), ((), ())), preferred...  68.9 us
    dot_general x5, matrix products, on_device(): jnp.dot(head_delta, local_in, preferred_element_type=jnp.float32)  53.4 us
    ppermute x5, waiting for transfers between devices, gather_around(): from_right = lax.ppermute(from_right, axis, behind)  42.7 us
  transfers between devices with their start and end apart: 34, of which 28 were waited for; matrix products, arithmetic and copies ran while one was open for 27% of the time, Pallas kernels for 0%

profile of v1, /device:TPU:0, one launch (start us, length us, event | category | flops | bytes accessed | tf_op | source)
XLA Modules:
  0.0 784.1 jit_solution(11475580243056568774)
XLA Ops:
  39.6 14.0 %fusion.37 = bf16[128,1536]{1,0:T(8,128)(2,1)} fusion(bf16[128,6144]{1,0:T(8,128)(2,1)S(1)} %constant_dynamic-update-slice_fusion.16, bf16[1,1536,6144]{2,1,0:T(8,128)(2,1)} %param.9), kind=kOutput, calls=%fused_computation.29 | convolution fusion | flops 2416115712 | bytes 20840448 | tf_op jit(solution)/shard_map/dot_general | solution.py:73
  63.3 15.6 %all-reduce.6.cloned.1.call-done = bf16[128,1536]{1,0:T(8,128)(2,1)} async-done(((bf16[128,1536]{1,0:T(8,128)(2,1)}), bf16[128,1536]{1,0:T(8,128)(2,1)}) %all-reduce.6.cloned.1.call-update) | async-done | bytes 393232 | tf_op jit(solution)/shard_map/psum | solution.py:76
  78.9 10.7 %fusion.22 = bf16[128,6144]{1,0:T(8,128)(2,1)} fusion(bf16[1,1536,6144]{2,1,0:T(8,128)(2,1)} %param.8, bf16[128,1536]{1,0:T(8,128)(2,1)} %all-reduce.6.cloned.1.call-done, bf16[1,1,128,1536]{3,2,1,0:T(8,128)(2,1)S(1)} %all-gather), kind=kOutput, calls=%fused_computation.24 | convolution fusion | flops 2420834304 | bytes 21233664 | tf_op jit(solution)/shard_map/dot_general | solution.py:81
  89.7 35.5 %reduce-scatter.6.cloned.1.call-done = bf16[128,1536]{1,0:T(8,128)(2,1)} async-done(((bf16[128,6144]{1,0:T(8,128)(2,1)}), bf16[128,1536]{1,0:T(8,128)(2,1)}) %reduce-scatter.6.cloned.1.call-update) | async-done | bytes 393232 | tf_op jit(solution)/shard_map/reduce_scatter | solution.py:82
  157.8 13.5 %fusion.40 = bf16[128,1536]{1,0:T(8,128)(2,1)} fusion(bf16[128,6144]{1,0:T(8,128)(2,1)S(1)} %constant_dynamic-update-slice_fusion.12, bf16[1,1536,6144]{2,1,0:T(8,128)(2,1)} %param.9), kind=kOutput, calls=%fused_computation.30 | convolution fusion | flops 2416115712 | bytes 20840448 | tf_op jit(solution)/shard_map/dot_general | solution.py:73
  177.7 21.9 %all-reduce.8.cloned.1.call-done = bf16[128,1536]{1,0:T(8,128)(2,1)} async-done(((bf16[128,1536]{1,0:T(8,128)(2,1)}), bf16[128,1536]{1,0:T(8,128)(2,1)}) %all-reduce.8.cloned.1.call-update) | async-done | bytes 393232 | tf_op jit(solution)/shard_map/psum | solution.py:76
  199.6 10.7 %fusion.25 = bf16[128,6144]{1,0:T(8,128)(2,1)} fusion(bf16[1,1536,6144]{2,1,0:T(8,128)(2,1)} %param.8, bf16[128,1536]{1,0:T(8,128)(2,1)} %all-reduce.8.cloned.1.call-done, bf16[1,1,128,1536]{3,2,1,0:T(8,128)(2,1)S(1)} %all-gather.2), kind=kOutput, calls=%fused_computation.25 | convolution fusion | flops 2420834304 | bytes 21233664 | tf_op jit(solution)/shard_map/dot_general | solution.py:81
  210.4 35.5 %reduce-scatter.8.cloned.1.call-done = bf16[128,1536]{1,0:T(8,128)(2,1)} async-done(((bf16[128,6144]{1,0:T(8,128)(2,1)}), bf16[128,1536]{1,0:T(8,128)(2,1)}) %reduce-scatter.8.cloned.1.call-update) | async-done | bytes 393232 | tf_op jit(solution)/shard_map/reduce_scatter | solution.py:82
  277.3 14.0 %fusion.43 = bf16[128,1536]{1,0:T(8,128)(2,1)} fusion(bf16[128,6144]{1,0:T(8,128)(2,1)S(1)} %constant_dynamic-update-slice_fusion.8, bf16[1,1536,6144]{2,1,0:T(8,128)(2,1)} %param.9), kind=kOutput, calls=%fused_computation.31 | convolution fusion | flops 2416115712 | bytes 20840448 | tf_op jit(solution)/shard_map/dot_general | solution.py:73
  297.9 21.4 %all-reduce.10.cloned.1.call-done = bf16[128,1536]{1,0:T(8,128)(2,1)} async-done(((bf16[128,1536]{1,0:T(8,128)(2,1)}), bf16[128,1536]{1,0:T(8,128)(2,1)}) %all-reduce.10.cloned.1.call-update) | async-done | bytes 393232 | tf_op jit(solution)/shard_map/psum | solution.py:76
  319.3 10.7 %fusion.28 = bf16[128,6144]{1,0:T(8,128)(2,1)} fusion(bf16[1,1536,6144]{2,1,0:T(8,128)(2,1)} %param.8, bf16[128,1536]{1,0:T(8,128)(2,1)} %all-reduce.10.cloned.1.call-done, bf16[1,1,128,1536]{3,2,1,0:T(8,128)(2,1)S(1)} %all-gather.4), kind=kOutput, calls=%fused_computation.26 | convolution fusion | flops 2420834304 | bytes 21233664 | tf_op jit(solution)/shard_map/dot_general | solution.py:81
  331.1 34.5 %reduce-scatter.10.cloned.1.call-done = bf16[128,1536]{1,0:T(8,128)(2,1)} async-done(((bf16[128,6144]{1,0:T(8,128)(2,1)}), bf16[128,1536]{1,0:T(8,128)(2,1)}) %reduce-scatter.10.cloned.1.call-update) | async-done | bytes 393232 | tf_op jit(solution)/shard_map/reduce_scatter | solution.py:82
  380.7 10.0 %collective-permute-done.13 = bf16[128,1536]{1,0:T(8,128)(2,1)S(1)} collective-permute-done((bf16[128,1536]{1,0:T(8,128)(2,1)S(1)}, bf16[128,1536]{1,0:T(8,128)(2,1)S(1)}, u32[]{:S(2)}, u32[]{:S(2)}) %collective-permute-start.13) | collective-permute-done | bytes 393248 | tf_op jit(solution)/shard_map/ppermute | solution.py:22
  397.0 14.0 %fusion.46 = bf16[128,1536]{1,0:T(8,128)(2,1)} fusion(bf16[128,6144]{1,0:T(8,128)(2,1)S(1)} %constant_dynamic-update-slice_fusion.4, bf16[1,1536,6144]{2,1,0:T(8,128)(2,1)} %param.9), kind=kOutput, calls=%fused_computation.32 | convolution fusion | flops 2416115712 | bytes 20840448 | tf_op jit(solution)/shard_map/dot_general | solution.py:73
  417.6 21.5 %all-reduce.12.cloned.1.call-done = bf16[128,1536]{1,0:T(8,128)(2,1)} async-done(((bf16[128,1536]{1,0:T(8,128)(2,1)}), bf16[128,1536]{1,0:T(8,128)(2,1)}) %all-reduce.12.cloned.1.call-update) | async-done | bytes 393232 | tf_op jit(solution)/shard_map/psum | solution.py:76
  439.1 10.7 %fusion.31 = bf16[128,6144]{1,0:T(8,128)(2,1)} fusion(bf16[1,1536,6144]{2,1,0:T(8,128)(2,1)} %param.8, bf16[128,1536]{1,0:T(8,128)(2,1)} %all-reduce.12.cloned.1.call-done, bf16[1,1,128,1536]{3,2,1,0:T(8,128)(2,1)S(1)} %all-gather.6), kind=kOutput, calls=%fused_computation.27 | convolution fusion | flops 2420834304 | bytes 21233664 | tf_op jit(solution)/shard_map/dot_general | solution.py:81
  453.7 31.7 %reduce-scatter.12.cloned.1.call-done = bf16[128,1536]{1,0:T(8,128)(2,1)} async-done(((bf16[128,6144]{1,0:T(8,128)(2,1)}), bf16[128,1536]{1,0:T(8,128)(2,1)}) %reduce-scatter.12.cloned.1.call-update) | async-done | bytes 393232 | tf_op jit(solution)/shard_map/reduce_scatter | solution.py:82
  496.6 16.6 %collective-permute-done.16 = bf16[128,1536]{1,0:T(8,128)(2,1)S(1)} collective-permute-done((bf16[128,1536]{1,0:T(8,128)(2,1)S(1)}, bf16[128,1536]{1,0:T(8,128)(2,1)S(1)}, u32[]{:S(2)}, u32[]{:S(2)}) %collective-permute-start.16) | collective-permute-done | bytes 393248 | tf_op jit(solution)/shard_map/ppermute | solution.py:17
  528.2 18.7 %collective-permute-done.18 = bf16[128,1536]{1,0:T(8,128)(2,1)S(1)} collective-permute-done((bf16[128,1536]{1,0:T(8,128)(2,1)S(1)}, bf16[128,1536]{1,0:T(8,128)(2,1)S(1)}, u32[]{:S(2)}, u32[]{:S(2)}) %collective-permute-start.18) | collective-permute-done | bytes 393248 | tf_op jit(solution)/shard_map/ppermute | solution.py:17
  546.9 13.5 %fusion.49 = bf16[128,1536]{1,0:T(8,128)(2,1)} fusion(bf16[128,6144]{1,0:T(8,128)(2,1)S(1)} %constant_dynamic-update-slice_fusion, bf16[1,1536,6144]{2,1,0:T(8,128)(2,1)} %param.9), kind=kOutput, calls=%fused_computation.33 | convolution fusion | flops 2416115712 | bytes 20840448 | tf_op jit(solution)/shard_map/dot_general | solution.py:73
  570.0 16.1 %fusion.116 = f32[1536,6144]{1,0:T(8,128)} fusion(bf16[128,6144]{1,0:T(8,128)(2,1)} %copy-done.4, bf16[1,1,128,1536]{3,2,1,0:T(8,128)(2,1)S(1)} %all-gather), kind=kOutput, calls=%fused_computation.138 | convolution fusion | flops 2417885184 | bytes 39714816 | tf_op jit(solution)/shard_map/dot_general | solution.py:86
  586.1 16.7 %fusion.59 = f32[1536,6144]{1,0:T(8,128)} fusion(bf16[1,1,128,6144]{3,2,1,0:T(8,128)(2,1)} %all-gather.16.cloned.1.call-done, bf16[128,1536]{1,0:T(8,128)(2,1)} %all-reduce.6.cloned.1.call-done, bf16[1,1,128,1536]{3,2,1,0:T(8,128)(2,1)S(1)} %all-gather), kind=kOutput, calls=%fused_computation.76 | convolution fusion | flops 2420047872 | bytes 40108032 | tf_op jit(solution)/shard_map/dot_general | solution.py:89
  602.8 14.9 %fusion.118 = f32[1536,6144]{1,0:T(8,128)} fusion(bf16[128,6144]{1,0:T(8,128)(2,1)S(1)} %constant_dynamic-update-slice_fusion.12, bf16[1,1,128,1536]{3,2,1,0:T(8,128)(2,1)S(1)} %copy-done.17), kind=kOutput, calls=%fused_computation.139 | convolution fusion | flops 2417885184 | bytes 39714816 | tf_op jit(solution)/shard_map/dot_general | solution.py:86
  617.7 17.0 %fusion.57 = f32[1536,6144]{1,0:T(8,128)} fusion(bf16[1,1,128,6144]{3,2,1,0:T(8,128)(2,1)} %all-gather.18.cloned.1.call-done, bf16[128,1536]{1,0:T(8,128)(2,1)} %all-reduce.8.cloned.1.call-done, bf16[1,1,128,1536]{3,2,1,0:T(8,128)(2,1)S(1)} %copy-done.18), kind=kOutput, calls=%fused_computation.74 | convolution fusion | flops 2420047872 | bytes 40108032 | tf_op jit(solution)/shard_map/dot_general | solution.py:89
  634.7 15.3 %fusion.120 = f32[1536,6144]{1,0:T(8,128)} fusion(bf16[128,6144]{1,0:T(8,128)(2,1)S(1)} %copy-done.1, bf16[1,1,128,1536]{3,2,1,0:T(8,128)(2,1)S(1)} %copy-done.20), kind=kOutput, calls=%fused_computation.140 | convolution fusion | flops 2417885184 | bytes 39714816 | tf_op jit(solution)/shard_map/dot_general | solution.py:86
  650.0 16.7 %fusion.55 = f32[1536,6144]{1,0:T(8,128)} fusion(bf16[1,1,128,6144]{3,2,1,0:T(8,128)(2,1)} %all-gather.20.cloned.1.call-done, bf16[128,1536]{1,0:T(8,128)(2,1)} %all-reduce.10.cloned.1.call-done, bf16[1,1,128,1536]{3,2,1,0:T(8,128)(2,1)S(1)} %copy-done.21), kind=kOutput, calls=%fused_computation.72 | convolution fusion | flops 2420047872 | bytes 40108032 | tf_op jit(solution)/shard_map/dot_general | solution.py:89
  666.7 15.0 %fusion.122 = f32[1536,6144]{1,0:T(8,128)} fusion(bf16[128,6144]{1,0:T(8,128)(2,1)S(1)} %copy-done.3, bf16[1,1,128,1536]{3,2,1,0:T(8,128)(2,1)S(1)} %copy-done.23), kind=kOutput, calls=%fused_computation.141 | convolution fusion | flops 2417885184 | bytes 39714816 | tf_op jit(solution)/shard_map/dot_general | solution.py:86
  681.7 17.0 %fusion.53 = f32[1536,6144]{1,0:T(8,128)} fusion(bf16[1,1,128,6144]{3,2,1,0:T(8,128)(2,1)} %all-gather.22.cloned.1.call-done, bf16[128,1536]{1,0:T(8,128)(2,1)} %all-reduce.12.cloned.1.call-done, bf16[1,1,128,1536]{3,2,1,0:T(8,128)(2,1)S(1)} %copy-done.24), kind=kOutput, calls=%fused_computation.70 | convolution fusion | flops 2420047872 | bytes 40108032 | tf_op jit(solution)/shard_map/dot_general | solution.py:89
  699.6 24.9 %fusion.1 = bf16[1,1536,6144]{2,1,0:T(8,128)(2,1)} fusion(bf16[128,6144]{1,0:T(8,128)(2,1)S(1)} %constant_dynamic-update-slice_fusion, f32[1536,6144]{1,0:T(8,128)} %fusion.122, f32[1536,6144]{1,0:T(8,128)} %fusion.120, f32[1536,6144]{1,0:T(8,128)} %fusion.118, f32[1536,6144]{1,0:T(8,128)} %fusion.116, pred[]{:T(512)S(6)} %and.49, pred[]{:T(512)S(6)} %and.48, ...), kind=kOutput, calls=%fused_computation.3 | convolution fusion | flops 2512257024 | bytes 171835392 | tf_op jit(solution)/shard_map/dot_general | solution.py:86
  724.6 10.7 %fusion.34 = bf16[128,6144]{1,0:T(8,128)(2,1)} fusion(bf16[1,1536,6144]{2,1,0:T(8,128)(2,1)} %param.8, bf16[128,1536]{1,0:T(8,128)(2,1)} %all-reduce.14.cloned.1.call-done, bf16[1,1,128,1536]{3,2,1,0:T(8,128)(2,1)S(1)} %copy-done.25), kind=kOutput, calls=%fused_computation.28 | convolution fusion | flops 2420834304 | bytes 21233664 | tf_op jit(solution)/shard_map/dot_general | solution.py:81
  736.3 25.8 %fusion = bf16[1,1536,6144]{2,1,0:T(8,128)(2,1)} fusion(f32[1536,6144]{1,0:T(8,128)} %fusion.53, f32[1536,6144]{1,0:T(8,128)} %fusion.55, f32[1536,6144]{1,0:T(8,128)} %fusion.57, f32[1536,6144]{1,0:T(8,128)} %fusion.59, pred[]{:T(512)S(6)} %and.49, pred[]{:T(512)S(6)} %and.48, pred[]{:T(512)S(6)} %and.47, pred[]{:T(512)S(6)} %and.46, pred[]{:T(512)S(6)} %and.42, ...), kind=kOutput, calls=%fused_computation.2 | convolution fusion | flops 2514419712 | bytes 172228608 | tf_op jit(solution)/shard_map/dot_general | solution.py:89
  762.1 13.2 %reduce-scatter.14.cloned.1.call-done = bf16[128,1536]{1,0:T(8,128)(2,1)} async-done(((bf16[128,6144]{1,0:T(8,128)(2,1)}), bf16[128,1536]{1,0:T(8,128)(2,1)}) %reduce-scatter.14.cloned.1.call-update) | async-done | bytes 393232 | tf_op jit(solution)/shard_map/reduce_scatter | solution.py:82
  (189 shorter events, 191.4 us)
Async XLA Ops:
  7.2 71.7 %all-reduce.6.cloned.1.call-start = ((), (), s32[]{:S(2)}) async-start(), calls=%async_computation.5 | async-start | bytes 786432 | tf_op jit(solution)/shard_map/psum | solution.py:76
  8.4 15.1 %collective-permute-start = (bf16[128,1536]{1,0:T(8,128)(2,1)S(1)}, bf16[128,1536]{1,0:T(8,128)(2,1)S(1)}, u32[]{:S(2)}, u32[]{:S(2)}) collective-permute-start(bf16[128,1536]{1,0:T(8,128)(2,1)S(1)} %get-tuple-element.20), channel_id=1, source_target_pairs={{0,1},{1,2},{2,3},{3,0},{4,5},{5,6},{6,7},{7,4},{8,9},{9,10},{10,1... | collective-permute-start | bytes 1179656 | tf_op jit(solution)/shard_map/ppermute | solution.py:17
  11.5 19.2 %collective-permute-start.1 = (bf16[128,1536]{1,0:T(8,128)(2,1)S(1)}, bf16[128,1536]{1,0:T(8,128)(2,1)S(1)}, u32[]{:S(2)}, u32[]{:S(2)}) collective-permute-start(bf16[128,1536]{1,0:T(8,128)(2,1)S(1)} %get-tuple-element.20), channel_id=1, source_target_pairs={{0,3},{1,0},{2,1},{3,2},{4,7},{5,4},{6,5},{7,6},{8,11},{9,8},{10,9... | collective-permute-start | bytes 1179656 | tf_op jit(solution)/shard_map/ppermute | solution.py:22
  23.5 16.0 %collective-permute-start.2 = (bf16[128,1536]{1,0:T(8,128)(2,1)S(1)}, bf16[128,1536]{1,0:T(8,128)(2,1)S(1)}, u32[]{:S(2)}, u32[]{:S(2)}) collective-permute-start(bf16[128,1536]{1,0:T(8,128)(2,1)S(1)} %collective-permute-done), channel_id=1, source_target_pairs={{0,1},{1,2},{2,3},{3,0},{4,5},{5,6},{6,7},{7,4},{8,9},{9,10},{10,1... | collective-permute-start | bytes 1179656 | tf_op jit(solution)/shard_map/ppermute | solution.py:17
  53.6 71.6 %reduce-scatter.6.cloned.1.call-start = ((), (), s32[]{:S(2)}) async-start(), calls=%async_computation.6 | async-start | bytes 1966080 | tf_op jit(solution)/shard_map/reduce_scatter | solution.py:82
  89.6 110.0 %all-reduce.8.cloned.1.call-start = ((), (), s32[]{:S(2)}) async-start(), calls=%async_computation.7 | async-start | bytes 786432 | tf_op jit(solution)/shard_map/psum | solution.py:76
  126.5 3.7 collective-permute-start.3
  131.5 9.7 %collective-permute-start.4 = (bf16[128,1536]{1,0:T(8,128)(2,1)S(1)}, bf16[128,1536]{1,0:T(8,128)(2,1)S(1)}, u32[]{:S(2)}, u32[]{:S(2)}) collective-permute-start(bf16[128,1536]{1,0:T(8,128)(2,1)S(1)} %get-tuple-element.18), channel_id=1, source_target_pairs={{0,1},{1,2},{2,3},{3,0},{4,5},{5,6},{6,7},{7,4},{8,9},{9,10},{10,1... | collective-permute-start | bytes 1179656 | tf_op jit(solution)/shard_map/ppermute | solution.py:17
  131.7 19.6 %collective-permute-start.5 = (bf16[128,1536]{1,0:T(8,128)(2,1)S(1)}, bf16[128,1536]{1,0:T(8,128)(2,1)S(1)}, u32[]{:S(2)}, u32[]{:S(2)}) collective-permute-start(bf16[128,1536]{1,0:T(8,128)(2,1)S(1)} %get-tuple-element.18), channel_id=1, source_target_pairs={{0,3},{1,0},{2,1},{3,2},{4,7},{5,4},{6,5},{7,6},{8,11},{9,8},{10,9... | collective-permute-start | bytes 1179656 | tf_op jit(solution)/shard_map/ppermute | solution.py:22
  141.3 16.5 %collective-permute-start.6 = (bf16[128,1536]{1,0:T(8,128)(2,1)S(1)}, bf16[128,1536]{1,0:T(8,128)(2,1)S(1)}, u32[]{:S(2)}, u32[]{:S(2)}) collective-permute-start(bf16[128,1536]{1,0:T(8,128)(2,1)S(1)} %collective-permute-done.4), channel_id=1, source_target_pairs={{0,1},{1,2},{2,3},{3,0},{4,5},{5,6},{6,7},{7,4},{8,9},{9,10},{10,1... | collective-permute-start | bytes 1179656 | tf_op jit(solution)/shard_map/ppermute | solution.py:17
  171.3 74.6 %reduce-scatter.8.cloned.1.call-start = ((), (), s32[]{:S(2)}) async-start(), calls=%async_computation.8 | async-start | bytes 1966080 | tf_op jit(solution)/shard_map/reduce_scatter | solution.py:82
  210.3 109.0 %all-reduce.10.cloned.1.call-start = ((), (), s32[]{:S(2)}) async-start(), calls=%async_computation.9 | async-start | bytes 786432 | tf_op jit(solution)/shard_map/psum | solution.py:76
  251.1 9.7 %collective-permute-start.8 = (bf16[128,1536]{1,0:T(8,128)(2,1)S(1)}, bf16[128,1536]{1,0:T(8,128)(2,1)S(1)}, u32[]{:S(2)}, u32[]{:S(2)}) collective-permute-start(bf16[128,1536]{1,0:T(8,128)(2,1)S(1)} %get-tuple-element.16), channel_id=1, source_target_pairs={{0,1},{1,2},{2,3},{3,0},{4,5},{5,6},{6,7},{7,4},{8,9},{9,10},{10,1... | collective-permute-start | bytes 1179656 | tf_op jit(solution)/shard_map/ppermute | solution.py:17
  251.3 19.8 %collective-permute-start.9 = (bf16[128,1536]{1,0:T(8,128)(2,1)S(1)}, bf16[128,1536]{1,0:T(8,128)(2,1)S(1)}, u32[]{:S(2)}, u32[]{:S(2)}) collective-permute-start(bf16[128,1536]{1,0:T(8,128)(2,1)S(1)} %get-tuple-element.16), channel_id=1, source_target_pairs={{0,3},{1,0},{2,1},{3,2},{4,7},{5,4},{6,5},{7,6},{8,11},{9,8},{10,9... | collective-permute-start | bytes 1179656 | tf_op jit(solution)/shard_map/ppermute | solution.py:22
  260.8 16.4 %collective-permute-start.10 = (bf16[128,1536]{1,0:T(8,128)(2,1)S(1)}, bf16[128,1536]{1,0:T(8,128)(2,1)S(1)}, u32[]{:S(2)}, u32[]{:S(2)}) collective-permute-start(bf16[128,1536]{1,0:T(8,128)(2,1)S(1)} %collective-permute-done.8), channel_id=1, source_target_pairs={{0,1},{1,2},{2,3},{3,0},{4,5},{5,6},{6,7},{7,4},{8,9},{9,10},{10,1... | collective-permute-start | bytes 1179656 | tf_op jit(solution)/shard_map/ppermute | solution.py:17
  291.3 74.3 %reduce-scatter.10.cloned.1.call-start = ((), (), s32[]{:S(2)}) async-start(), calls=%async_computation.10 | async-start | bytes 1966080 | tf_op jit(solution)/shard_map/reduce_scatter | solution.py:82
  330.0 109.1 %all-reduce.12.cloned.1.call-start = ((), (), s32[]{:S(2)}) async-start(), calls=%async_computation.11 | async-start | bytes 786432 | tf_op jit(solution)/shard_map/psum | solution.py:76
  370.8 9.7 %collective-permute-start.12 = (bf16[128,1536]{1,0:T(8,128)(2,1)S(1)}, bf16[128,1536]{1,0:T(8,128)(2,1)S(1)}, u32[]{:S(2)}, u32[]{:S(2)}) collective-permute-start(bf16[128,1536]{1,0:T(8,128)(2,1)S(1)} %get-tuple-element.14), channel_id=1, source_target_pairs={{0,1},{1,2},{2,3},{3,0},{4,5},{5,6},{6,7},{7,4},{8,9},{9,10},{10,1... | collective-permute-start | bytes 1179656 | tf_op jit(solution)/shard_map/ppermute | solution.py:17
  371.0 19.8 %collective-permute-start.13 = (bf16[128,1536]{1,0:T(8,128)(2,1)S(1)}, bf16[128,1536]{1,0:T(8,128)(2,1)S(1)}, u32[]{:S(2)}, u32[]{:S(2)}) collective-permute-start(bf16[128,1536]{1,0:T(8,128)(2,1)S(1)} %get-tuple-element.14), channel_id=1, source_target_pairs={{0,3},{1,0},{2,1},{3,2},{4,7},{5,4},{6,5},{7,6},{8,11},{9,8},{10,9... | collective-permute-start | bytes 1179656 | tf_op jit(solution)/shard_map/ppermute | solution.py:22
  380.5 16.4 %collective-permute-start.14 = (bf16[128,1536]{1,0:T(8,128)(2,1)S(1)}, bf16[128,1536]{1,0:T(8,128)(2,1)S(1)}, u32[]{:S(2)}, u32[]{:S(2)}) collective-permute-start(bf16[128,1536]{1,0:T(8,128)(2,1)S(1)} %collective-permute-done.12), channel_id=1, source_target_pairs={{0,1},{1,2},{2,3},{3,0},{4,5},{5,6},{6,7},{7,4},{8,9},{9,10},{10,1... | collective-permute-start | bytes 1179656 | tf_op jit(solution)/shard_map/ppermute | solution.py:17
  411.0 74.4 %reduce-scatter.12.cloned.1.call-start = ((), (), s32[]{:S(2)}) async-start(), calls=%async_computation.12 | async-start | bytes 1966080 | tf_op jit(solution)/shard_map/reduce_scatter | solution.py:82
  449.8 136.3 %all-gather.16.cloned.1.call-start = ((), (), s32[]{:S(2)}) async-start(), calls=%async_computation.15 | async-start | bytes 1966080 | tf_op jit(solution)/shard_map/all_gather | solution.py:71
  452.2 165.4 %all-gather.18.cloned.1.call-start = ((), (), s32[]{:S(2)}) async-start(), calls=%async_computation.16 | async-start | bytes 1966080 | tf_op jit(solution)/shard_map/all_gather | solution.py:71
  452.8 197.1 %all-gather.20.cloned.1.call-start = ((), (), s32[]{:S(2)}) async-start(), calls=%async_computation.17 | async-start | bytes 1966080 | tf_op jit(solution)/shard_map/all_gather | solution.py:71
  453.6 228.1 %all-gather.22.cloned.1.call-start = ((), (), s32[]{:S(2)}) async-start(), calls=%async_computation.18 | async-start | bytes 1966080 | tf_op jit(solution)/shard_map/all_gather | solution.py:71
  487.3 3.9 collective-permute-start.15
  488.6 236.0 %all-reduce.14.cloned.1.call-start = ((), (), s32[]{:S(2)}) async-start(), calls=%async_computation.13 | async-start | bytes 786432 | tf_op jit(solution)/shard_map/psum | solution.py:76
  492.7 20.5 %collective-permute-start.16 = (bf16[128,1536]{1,0:T(8,128)(2,1)S(1)}, bf16[128,1536]{1,0:T(8,128)(2,1)S(1)}, u32[]{:S(2)}, u32[]{:S(2)}) collective-permute-start(bf16[128,1536]{1,0:T(8,128)(2,1)S(1)} %get-tuple-element.12), channel_id=1, source_target_pairs={{0,1},{1,2},{2,3},{3,0},{4,5},{5,6},{6,7},{7,4},{8,9},{9,10},{10,1... | collective-permute-start | bytes 1179656 | tf_op jit(solution)/shard_map/ppermute | solution.py:17
  492.9 35.3 %collective-permute-start.17 = (bf16[128,1536]{1,0:T(8,128)(2,1)S(1)}, bf16[128,1536]{1,0:T(8,128)(2,1)S(1)}, u32[]{:S(2)}, u32[]{:S(2)}) collective-permute-start(bf16[128,1536]{1,0:T(8,128)(2,1)S(1)} %get-tuple-element.12), channel_id=1, source_target_pairs={{0,3},{1,0},{2,1},{3,2},{4,7},{5,4},{6,5},{7,6},{8,11},{9,8},{10,9... | collective-permute-start | bytes 1179656 | tf_op jit(solution)/shard_map/ppermute | solution.py:22
  513.2 33.7 %collective-permute-start.18 = (bf16[128,1536]{1,0:T(8,128)(2,1)S(1)}, bf16[128,1536]{1,0:T(8,128)(2,1)S(1)}, u32[]{:S(2)}, u32[]{:S(2)}) collective-permute-start(bf16[128,1536]{1,0:T(8,128)(2,1)S(1)} %collective-permute-done.16), channel_id=1, source_target_pairs={{0,1},{1,2},{2,3},{3,0},{4,5},{5,6},{6,7},{7,4},{8,9},{9,10},{10,1... | collective-permute-start | bytes 1179656 | tf_op jit(solution)/shard_map/ppermute | solution.py:17
  560.4 174.9 %all-gather.24.cloned.1.call-start = ((), (), s32[]{:S(2)}) async-start(), calls=%async_computation.19 | async-start | bytes 1966080 | tf_op jit(solution)/shard_map/all_gather | solution.py:71
  561.0 214.3 %reduce-scatter.14.cloned.1.call-start = ((), (), s32[]{:S(2)}) async-start(), calls=%async_computation.14 | async-start | bytes 1966080 | tf_op jit(solution)/shard_map/reduce_scatter | solution.py:82
  (40 other events, 578.6 us)
Sparse Core Ops, SparseCore 0:
  53.7 25.0 all-reduce.5
  89.7 35.4 reduce-scatter.5
  171.5 28.1 all-reduce.7
  210.4 35.4 reduce-scatter.7
  291.4 27.8 all-reduce.9
  330.1 35.4 reduce-scatter.9
  411.1 27.9 all-reduce.11
  449.9 35.4 reduce-scatter.11
  487.0 58.9 all-gather.15
  547.3 36.1 all-gather.17
  585.1 35.8 all-gather.19
  622.5 35.8 all-gather.21
  660.7 24.6 all-reduce.13
  686.8 37.0 all-gather.23
  735.4 39.8 reduce-scatter.13
